TPU v7x, 32 devices: a whole 2x2x4 slice. The times are simulated.
32 devices in a mesh: shot: 4 (over y, x), tile: 8 (over z, core).
Axes of the slice: x: 2, y: 2, z: 4, core: 2. Of those that a mesh axis runs over, the one named last changes fastest.
Arguments:
- p_now: float32 [4, 1024, 16, 128], P('shot', 'tile'), may hold values from -6 to 6
- p_prev: float32 [4, 1024, 16, 128], P('shot', 'tile'), may hold values from -6 to 6
- adj_now: float32 [4, 1024, 16, 128], P('shot', 'tile'), may hold values from -60 to 60
- adj_next: float32 [4, 1024, 16, 128], P('shot', 'tile'), may hold values from -60 to 60
- coef_old: float32 [512, 512], P('tile'), may hold values from 0.14 to 0.28
- signs: int32 [4, 512], P('shot', 'tile'), may hold values from 0 to 1
- elem_index: int32 [512], P('tile'), may hold values from 0 to 262143
- wavelet: float32 [5], replicated, may hold values from -4 to 4
Outputs:
- direction: float32 [512, 512], P('tile')
- p_last: float32 [4, 1024, 16, 128], P('shot', 'tile')
All inputs are finite; a program needn't handle non-finite values.
Results may differ from a plain program's by a relative error of at most 0.0003.
Values sent between devices are 32-bit elements; how exact they have to be, the bound alone decides.
A program may use at most 64 MiB of HBM per device.

v0:
```python
import functools

import jax
import jax.numpy as jnp
import ml_dtypes
import numpy as np
from jax import lax
from jax.experimental import pallas as pl
from jax.experimental.pallas import tpu as pltpu
from jax.sharding import PartitionSpec as P

OV = 8
LEARN = 0.02
EPSILON = 1e-06
F32 = jnp.float32
BF16 = jnp.bfloat16
MESH = pl.DeviceIdType.MESH


def spectral_second(length):
    index = np.arange(length)
    number = np.minimum(index, length - index) * (2.0 * np.pi / length)
    gap = (index[:, None] - index[None, :])[:, :, None] * index[None, None, :] % length
    return np.sum(-(number * number) / length * np.cos(2.0 * np.pi / length * gap), axis=-1)


def spline_weight(offset):
    mag = np.abs(offset)
    inner = 2.0 / 3.0 - mag * mag + 0.5 * mag * mag * mag
    outer = (2.0 - mag) ** 3 / 6.0
    return np.where(mag < 1.0, inner, np.where(mag < 2.0, outer, 0.0))


def periodic_spline(fine, coarse):
    gap = np.arange(fine)[:, None] - 2 * np.arange(coarse)[None, :]
    return sum(spline_weight((gap + image * fine - 0.5) * 0.5) for image in range(-2, 3))


def halves(matrix):
    high = matrix.astype(np.float32).astype(ml_dtypes.bfloat16)
    low = (matrix - high.astype(np.float64)).astype(ml_dtypes.bfloat16)
    return high, low


def twice(block):
    out = np.zeros((2 * block.shape[0], 2 * block.shape[1]))
    out[: block.shape[0], : block.shape[1]] = block
    out[block.shape[0] :, block.shape[1] :] = block
    return out


def constants(cx, cz, cxc, czc):
    full = cx + 2 * OV
    ramp = np.sin(0.5 * np.pi * (np.arange(OV) + 0.5) / OV) ** 2
    second_x = spectral_second(full)[OV : OV + cx]
    high, low = halves(second_x[:, OV : OV + cx])
    core_x = np.block([[high, high], [low, low]])
    rim = np.concatenate([second_x[:, :OV] * ramp, second_x[:, OV + cx :] * ramp[::-1]], 1)
    high, low = halves(rim)
    rim_x = np.block([[high, high], [low, low]])
    high, low = halves(spectral_second(cz))
    core_z = np.block([[high, low], [high, low]])
    gap = np.arange(cx)[:, None] - 2 * (np.arange(cxc + 2 * OV)[None, :] - OV)
    expand_x = spline_weight((gap - 0.5) * 0.5)
    spline_z = periodic_spline(cz, czc)
    floats = [expand_x, twice(spline_z.T), expand_x.T, twice(spline_z)]
    return [core_x, rim_x, core_z] + [m.astype(np.float32) for m in floats]


def split(value):
    high = value.astype(BF16)
    return high, (value - high.astype(F32)).astype(BF16)


def dot(a, b):
    return jnp.dot(a, b, preferred_element_type=F32)


def dot3(a, b):
    ah, al = split(a)
    bh, bl = split(b)
    return dot(ah, bh) + (dot(ah, bl) + dot(al, bh))


def kernel(
    dims, n_shot, n_tile, spline_y,
    p_now, p_prev, q_now, q_next, coef, signs, elems, wave,
    core_x, rim_x, core_z, exp_x, exp_z, pro_x, pro_z,
    direction, p_last,
    raw, raw_sem, pf, qf, lp, lq, sig, sig2, src, wide, exp_t,
    ph, qh, cext, narrow, part0, rims, part, rs, tot, ttot, sq_out, sq_in,
    ph_s, ph_r, qh_s, qh_r, ce_s, ce_r, ri_s, ri_r, rs_s, rs_r, ag_s, ag_r, sq_s, sq_r,
):
    cx, cy, cz, cxc, pairs, steps, group, rows = dims
    shot = lax.axis_index("shot")
    tile = lax.axis_index("tile")
    has_left = tile > 0
    has_right = tile < n_tile - 1
    ext = cxc + 2 * OV

    loads = []
    for i, ref in enumerate((p_now, q_now, p_prev, q_next)):
        copy = pltpu.make_async_copy(ref, raw.at[i], raw_sem.at[i])
        copy.start()
        loads.append(copy)

    barrier = pltpu.get_barrier_semaphore()
    for d in range(1, n_tile):
        pl.semaphore_signal(
            barrier, inc=1, device_id={"tile": lax.rem(tile + d, n_tile)}, device_id_type=MESH
        )
    for d in range(1, n_shot):
        pl.semaphore_signal(
            barrier, inc=1, device_id={"shot": lax.rem(shot + d, n_shot)}, device_id_type=MESH
        )

    def to_planes(i, out):
        loads[i].wait()
        for y in range(cy):
            out[y] = raw[i, pl.ds(y, cx, stride=cy), :]

    for a in range(pairs):
        cext[a, OV : OV + cxc, :] = coef[:, a * 128 : (a + 1) * 128]

    @pl.when(jnp.logical_not(has_left))
    def _():
        ph[:, 0] = jnp.zeros_like(ph[:, 0])
        qh[:, 0] = jnp.zeros_like(qh[:, 0])
        cext[:, :OV, :] = jnp.zeros((pairs, OV, 128), F32)
        rims[0] = jnp.zeros_like(rims[0])

    @pl.when(jnp.logical_not(has_right))
    def _():
        ph[:, 1] = jnp.zeros_like(ph[:, 1])
        qh[:, 1] = jnp.zeros_like(qh[:, 1])
        cext[:, OV + cxc :, :] = jnp.zeros((pairs, OV, 128), F32)
        rims[1] = jnp.zeros_like(rims[1])

    def beside(to_right, right_dst, to_left, left_dst, ss, rr):
        right = pltpu.make_async_remote_copy(
            src_ref=to_right, dst_ref=right_dst, send_sem=ss.at[0], recv_sem=rr.at[0],
            device_id={"tile": lax.rem(tile + 1, n_tile)}, device_id_type=MESH,
        )
        left = pltpu.make_async_remote_copy(
            src_ref=to_left, dst_ref=left_dst, send_sem=ss.at[1], recv_sem=rr.at[1],
            device_id={"tile": lax.rem(tile + n_tile - 1, n_tile)}, device_id_type=MESH,
        )
        return right, left

    def start(pair):
        @pl.when(has_right)
        def _():
            pair[0].start()

        @pl.when(has_left)
        def _():
            pair[1].start()

    def finish(pair):
        @pl.when(has_right)
        def _():
            pair[0].wait_send()
            pair[1].wait_recv()

        @pl.when(has_left)
        def _():
            pair[1].wait_send()
            pair[0].wait_recv()

    def field_halo(field, index, halo, t, ss, rr):
        return beside(
            field.at[index, :, cx - OV :, :], halo.at[t, 0],
            field.at[index, :, :OV, :], halo.at[t, 1], ss.at[t], rr.at[t],
        )

    p_halo = lambda t: field_halo(pf, t + 1, ph, t, ph_s, ph_r)
    q_halo = lambda t: field_halo(qf, t + 1, qh, t, qh_s, qh_r)

    to_planes(0, pf.at[1])
    pl.semaphore_wait(barrier, n_tile + n_shot - 2)
    start(p_halo(0))
    to_planes(1, qf.at[1])
    start(q_halo(0))
    coef_rims = beside(
        cext.at[:, cxc : cxc + OV, :], cext.at[:, :OV, :],
        cext.at[:, OV : 2 * OV, :], cext.at[:, OV + cxc :, :], ce_s, ce_r,
    )
    start(coef_rims)

    def core(field, out):
        def body(i, carry):
            y0 = 2 * i
            y1 = y0 + 1
            a = field[y0]
            b = field[y1]
            high, low = split(jnp.concatenate([a, b], 1))
            ox = dot(core_x[...], jnp.concatenate([high, low], 0))
            oz = dot(
                jnp.concatenate(
                    [
                        jnp.concatenate([high[:, :cz], low[:, :cz]], 1),
                        jnp.concatenate([high[:, cz:], low[:, cz:]], 1),
                    ],
                    0,
                ),
                core_z[...],
            )
            before = field[lax.rem(y0 + cy - 1, cy)]
            after = field[lax.rem(y1 + 1, cy)]
            ox = ox[:cx] + ox[cx:]
            oz = oz[:, :cz] + oz[:, cz:]
            out[y0] = ox[:, :cz] + (before + b - 2.0 * a) + oz[:cx]
            out[y1] = ox[:, cz:] + (a + after - 2.0 * b) + oz[cx:]
            return carry

        lax.fori_loop(0, cy // 2, body, 0, unroll=2)

    def with_rim(halo, lap, use):
        def body(i, carry):
            y0 = 2 * i
            y1 = y0 + 1
            edge = jnp.concatenate(
                [
                    jnp.concatenate([halo[0, y0], halo[0, y1]], 1),
                    jnp.concatenate([halo[1, y0], halo[1, y1]], 1),
                ],
                0,
            )
            ox = dot(rim_x[...], jnp.concatenate(split(edge), 0))
            ox = ox[:cx] + ox[cx:]
            use(y0, lap[y0] + ox[:, :cz])
            use(y1, lap[y1] + ox[:, cz:])
            return carry

        lax.fori_loop(0, cy // 2, body, 0, unroll=2)

    def expand(coefs, out):
        for a in range(pairs):
            both = dot3(dot3(exp_x[...], coefs[a]), exp_z[...])
            wide[2 * a] = both[:, :cz]
            wide[2 * a + 1] = both[:, cz:]

        def body(i, carry):
            at = pl.ds(pl.multiple_of(i * 8, 8), 8)
            planes = [wide[j, at, :] for j in range(2 * pairs)]
            for y in range(cy):
                terms = [
                    float(spline_y[y, j]) * planes[j] for j in range(2 * pairs) if spline_y[y, j] != 0
                ]
                out[y, at, :] = functools.reduce(lambda u, v: u + v, terms)
            return carry

        lax.fori_loop(0, cx // 8, body, 0)

    count = elems.shape[1]
    where_to = elems[...]
    amount = (2 * signs[...] - 1).astype(F32)
    row_of = lax.rem(lax.div(where_to, cz), cy) * cx + lax.div(where_to, cz * cy)
    lanes = (lax.broadcasted_iota(jnp.int32, (cz, count), 0) == lax.rem(where_to, cz)).astype(F32)
    lanes = lanes.astype(BF16)

    def source(y, carry):
        place = lax.broadcasted_iota(jnp.int32, (cx, count), 0) + y * cx
        hits = jnp.where(place == row_of, amount, 0.0).astype(BF16)
        src[y] = lax.dot_general(hits, lanes, (((1,), (1,)), ((), ())), preferred_element_type=F32)
        return carry

    lax.fori_loop(0, cy, source, 0, unroll=2)
    to_planes(2, pf.at[0])
    to_planes(3, qf.at[0])
    finish(coef_rims)
    expand(cext, sig)

    def square(y, carry):
        value = sig[y]
        sig2[y] = value * value
        return carry

    lax.fori_loop(0, cy, square, 0)

    def step(t, carry):
        core(pf.at[t + 1], lp.at[t])
        core(qf.at[t + 1], lq)
        finish(p_halo(t))
        scale = wave[t]

        def use_p(y, lap):
            lp[t, y] = lap
            pf[t + 2, y] = 2.0 * pf[t + 1, y] - pf[t, y] + sig2[y] * lap + scale * src[y]

        with_rim(ph.at[t], lp.at[t], use_p)
        start(p_halo(t + 1))
        finish(q_halo(t))

        def use_q(y, lap):
            qf[t + 2, y] = 2.0 * qf[t + 1, y] - qf[t, y] + sig2[y] * lap

        with_rim(qh.at[t], lq, use_q)

        @pl.when(t < steps - 1)
        def _():
            start(q_halo(t + 1))

        return carry

    lax.fori_loop(0, steps, step, 0)

    def image(i, carry):
        at = pl.ds(pl.multiple_of(i * 8, 8), 8)
        out = [None] * (2 * pairs)
        for y in range(cy):
            summed = qf[steps + 1, y, at, :] * lp[0, y, at, :]
            for t in range(1, steps):
                summed = summed + qf[steps + 1 - t, y, at, :] * lp[t, y, at, :]
            value = 2.0 * sig[y, at, :] * summed
            for j in range(2 * pairs):
                if spline_y[y, j] != 0:
                    term = float(spline_y[y, j]) * value
                    out[j] = term if out[j] is None else out[j] + term
        for j in range(2 * pairs):
            narrow[j, at, :] = out[j]
        return carry

    lax.fori_loop(0, cx // 8, image, 0)
    for a in range(pairs):
        both = jnp.concatenate([narrow[2 * a], narrow[2 * a + 1]], 1)
        part0[a] = dot3(dot3(pro_x[...], both), pro_z[...])
    part_rims = beside(
        part0.at[:, cxc:, :], rims.at[0], part0.at[:, : 2 * OV, :], rims.at[1], ri_s, ri_r
    )
    start(part_rims)
    core(pf.at[steps + 1], lp.at[steps])
    finish(part_rims)
    halfs = ext // rows
    for a in range(pairs):
        whole = jnp.concatenate(
            [
                part0[a, : 2 * OV, :] + rims[0, a],
                part0[a, 2 * OV : cxc, :],
                part0[a, cxc:, :] + rims[1, a],
            ],
            0,
        )
        for r in range(halfs):
            flat = a * halfs + r
            part[flat // group, flat % group] = whole[r * rows : (r + 1) * rows]

    def peer_copy(source_ref, target_ref, d, ss, rr):
        return pltpu.make_async_remote_copy(
            src_ref=source_ref, dst_ref=target_ref, send_sem=ss.at[d - 1], recv_sem=rr.at[d - 1],
            device_id={"shot": lax.rem(shot + d, n_shot)}, device_id_type=MESH,
        )

    scatter = []
    for d in range(1, n_shot):
        copy = peer_copy(part.at[lax.rem(shot + d, n_shot)], rs.at[d - 1], d, rs_s, rs_r)
        copy.start()
        scatter.append(copy)
    finish(p_halo(steps))

    def keep(y, lap):
        lp[steps, y] = lap

    with_rim(ph.at[steps], lp.at[steps], keep)
    mine = part[shot]
    for d in range(1, n_shot):
        scatter[d - 1].wait()
        mine = mine + rs[d - 1]
    tot[shot] = mine
    gather = []
    for d in range(1, n_shot):
        copy = peer_copy(tot.at[shot], tot.at[shot], d, ag_s, ag_r)
        copy.start()
        gather.append(copy)
    for copy in gather:
        copy.wait()
    left_on = jnp.where(has_left, 1.0, 0.0).astype(F32)
    right_on = jnp.where(has_right, 1.0, 0.0).astype(F32)
    squares = jnp.zeros((8, 128), F32)
    for a in range(pairs):
        pieces = []
        for r in range(halfs):
            flat = a * halfs + r
            pieces.append(tot[flat // group, flat % group])
        whole = pieces[0] if halfs == 1 else jnp.concatenate(pieces, 0)
        ttot[a, :OV, :] = whole[:OV] * left_on
        ttot[a, OV : OV + cxc, :] = whole[OV : OV + cxc]
        ttot[a, OV + cxc :, :] = whole[OV + cxc :] * right_on
        for r in range(OV, OV + cxc, 8):
            squares = squares + whole[r : r + 8] * whole[r : r + 8]
    sq_out[...] = squares
    sums = []
    for d in range(1, n_tile):
        copy = pltpu.make_async_remote_copy(
            src_ref=sq_out, dst_ref=sq_in.at[d - 1], send_sem=sq_s.at[d - 1], recv_sem=sq_r.at[d - 1],
            device_id={"tile": lax.rem(tile + d, n_tile)}, device_id_type=MESH,
        )
        copy.start()
        sums.append(copy)
    expand(ttot, exp_t)
    for copy in sums:
        copy.wait()
    for d in range(1, n_tile):
        squares = squares + sq_in[d - 1]
    cells = float(n_tile * cxc * 2 * pairs * 64)
    mean = jnp.sum(jnp.sum(squares, axis=0, keepdims=True), axis=1, keepdims=True) / cells
    scale = 1.0 / jnp.sqrt(mean + EPSILON)
    for a in range(pairs):
        direction[:, a * 128 : (a + 1) * 128] = ttot[a, OV : OV + cxc, :] * scale
    moved = LEARN * scale
    last = wave[steps]
    for y in range(cy):
        speed = sig[y] - moved * exp_t[y]
        p_last[pl.ds(y, cx, stride=cy), :] = (
            2.0 * pf[steps + 1, y] - pf[steps, y] + speed * speed * lp[steps, y] + last * src[y]
        )


def on_device(n_shot, n_tile, p_now, p_prev, adj_now, adj_next, coef_old, signs, elem_index, wavelet):
    _, cx, cy, cz = p_now.shape
    cxc, merged = coef_old.shape
    steps = wavelet.shape[0] - 1
    cyc = cy // 2
    czc = merged // cyc
    pairs = cyc // 2
    spline_y = periodic_spline(cy, cyc).astype(np.float32)
    ext = cxc + 2 * OV
    group = max(1, pairs // n_shot)
    rows = ext // max(1, n_shot // pairs)
    dims = (cx, cy, cz, cxc, pairs, steps, group, rows)
    flat = lambda v: v.reshape(cx * cy, cz)
    consts = [jnp.asarray(c) for c in constants(cx, cz, cxc, czc)]
    vmem = pl.BlockSpec(memory_space=pltpu.VMEM)
    field = (cy, cx, cz)
    buf = lambda *shape: pltpu.VMEM(shape, F32)
    sem = lambda *shape: pltpu.SemaphoreType.DMA(shape)
    direction, p_last = pl.pallas_call(
        functools.partial(kernel, dims, n_shot, n_tile, spline_y),
        out_shape=(
            jax.ShapeDtypeStruct((cxc, merged), F32),
            jax.ShapeDtypeStruct((cx * cy, cz), F32),
        ),
        in_specs=[pl.BlockSpec(memory_space=pl.ANY)] * 4
        + [vmem] * 3
        + [pl.BlockSpec(memory_space=pltpu.SMEM)]
        + [vmem] * len(consts),
        out_specs=(vmem, vmem),
        scratch_shapes=[
            buf(4, cx * cy, cz), sem(4),
            buf(steps + 2, *field), buf(steps + 2, *field), buf(steps + 1, *field), buf(*field),
            buf(*field), buf(*field), buf(*field), buf(cyc, cx, cz), buf(*field),
            buf(steps + 1, 2, cy, OV, cz), buf(steps, 2, cy, OV, cz),
            buf(pairs, ext, 128), buf(cyc, cx, cz), buf(pairs, ext, 128),
            buf(2, pairs, 2 * OV, 128),
            buf(n_shot, group, rows, 128), buf(max(1, n_shot - 1), group, rows, 128),
            buf(n_shot, group, rows, 128), buf(pairs, ext, 128),
            buf(8, 128), buf(max(1, n_tile - 1), 8, 128),
            sem(steps + 1, 2), sem(steps + 1, 2), sem(steps, 2), sem(steps, 2),
            sem(2), sem(2), sem(2), sem(2),
            sem(max(1, n_shot - 1)), sem(max(1, n_shot - 1)),
            sem(max(1, n_shot - 1)), sem(max(1, n_shot - 1)),
            sem(max(1, n_tile - 1)), sem(max(1, n_tile - 1)),
        ],
        compiler_params=pltpu.CompilerParams(
            collective_id=0, has_side_effects=True, vmem_limit_bytes=56 * 1024 * 1024
        ),
    )(
        flat(p_now), flat(p_prev), flat(adj_now), flat(adj_next), coef_old,
        signs, elem_index.reshape(1, -1), wavelet, *consts,
    )
    return direction, p_last.reshape(1, cx, cy, cz)


def solution(mesh):
    placed = (
        P("shot", "tile", None, None),
        P("shot", "tile", None, None),
        P("shot", "tile", None, None),
        P("shot", "tile", None, None),
        P("tile", None),
        P("shot", "tile"),
        P("tile"),
        P(),
    )
    return jax.shard_map(
        functools.partial(on_device, mesh.shape["shot"], mesh.shape["tile"]),
        mesh=mesh,
        in_specs=placed,
        out_specs=(P("tile", None), P("shot", "tile", None, None)),
        check_vma=False,
    )
```

profile of v0, /device:TPU:0, one launch (start us, length us, event | category | flops | bytes accessed | tf_op | source)
XLA Modules:
  0.0 52.5 jit_solution(16399820115341050998)
XLA Ops:
  0.6 48.1 %shard_map.158 = (f32[64,512]{1,0:T(8,128)}, f32[2048,128]{1,0:T(8,128)}) custom-call(f32[2048,128]{1,0:T(8,128)} %bitcast.7, f32[2048,128]{1,0:T(8,128)} %bitcast.8, f32[2048,128]{1,0:T(8,128)} %bitcast.9, f32[2048,128]{1,0:T(8,128)} %bitcast.10, f32[64,512]{1,0:T(8,128)} %coef.1, s32[1,64]{1,0:T(1,128)} %signs.1, s32[1,64]{1,0:T(1,128)} %bitcast.11, ...), custom_call_target="tpu_custom_call" | custom-call | tf_op jit(solution)/shard_map/pallas_call | solution.py:437
  48.7 1.6 %copy.19 = f32[64,512]{1,0:T(8,128)} copy(f32[64,512]{1,0:T(8,128)} %get-tuple-element.8) | data formatting | bytes 262144
  50.3 2.3 %copy.20 = f32[1,128,16,128]{3,2,1,0:T(8,128)} copy(f32[1,128,16,128]{3,2,1,0:T(8,128)} %bitcast.6) | data formatting | bytes 2097152
where the time goes:
time: 52.7 us; the launch traced here: 52.5 us
  Pallas kernels  48.1 us (91%)
  local copies, waits for them, and re-layouts  3.83 us (7%)
  between operations  0.64 us (1%)
    pallas_call x1, Pallas kernels, on_device(): pl.pallas_call(functools.partial(kernel, dims, n_shot, n_tile, spline_y),...  48.1 us
    unnamed x2, local copies, waits for them, and re-layouts  3.83 us

commit v1 on v0

--- a/solution.py
+++ b/solution.py
@@ -84,12 +84,13 @@
 
 def kernel(
     dims, n_shot, n_tile, spline_y,
-    p_now, p_prev, q_now, q_next, coef, signs, elems, wave,
-    core_x, rim_x, core_z, exp_x, exp_z, pro_x, pro_z,
+    p_now, p_prev, q_now, q_next, coef_in, signs, elems, wave,
+    core_x_in, rim_x_in, core_z_in, exp_x_in, exp_z_in, pro_x_in, pro_z_in,
     direction, p_last,
     raw, raw_sem, pf, qf, lp, lq, sig, sig2, src, wide, exp_t,
     ph, qh, cext, narrow, part0, rims, part, rs, tot, ttot, sq_out, sq_in,
     ph_s, ph_r, qh_s, qh_r, ce_s, ce_r, ri_s, ri_r, rs_s, rs_r, ag_s, ag_r, sq_s, sq_r,
+    sq_all, sa_s, sa_r, consts_sem, coef, core_x, rim_x, core_z, exp_x, exp_z, pro_x, pro_z,
 ):
     cx, cy, cz, cxc, pairs, steps, group, rows = dims
     shot = lax.axis_index("shot")
@@ -98,12 +99,6 @@
     has_right = tile < n_tile - 1
     ext = cxc + 2 * OV
 
-    loads = []
-    for i, ref in enumerate((p_now, q_now, p_prev, q_next)):
-        copy = pltpu.make_async_copy(ref, raw.at[i], raw_sem.at[i])
-        copy.start()
-        loads.append(copy)
-
     barrier = pltpu.get_barrier_semaphore()
     for d in range(1, n_tile):
         pl.semaphore_signal(
@@ -114,13 +109,26 @@
             barrier, inc=1, device_id={"shot": lax.rem(shot + d, n_shot)}, device_id_type=MESH
         )
 
+    def load(ref, out, s):
+        copy = pltpu.make_async_copy(ref, out, s)
+        copy.start()
+        return copy
+
+    fields = (p_now, q_now, p_prev, q_next)
+    matrices = (
+        (core_x_in, core_x), (core_z_in, core_z), (rim_x_in, rim_x), (exp_x_in, exp_x),
+        (exp_z_in, exp_z), (pro_x_in, pro_x), (pro_z_in, pro_z),
+    )
+    loads = [load(fields[0], raw.at[0], raw_sem.at[0])]
+    coef_load = load(coef_in, coef, consts_sem.at[0])
+    loads.append(load(fields[1], raw.at[1], raw_sem.at[1]))
+    matrix_loads = [load(a, b, consts_sem.at[i + 1]) for i, (a, b) in enumerate(matrices)]
+    loads += [load(fields[i], raw.at[i], raw_sem.at[i]) for i in (2, 3)]
+
     def to_planes(i, out):
         loads[i].wait()
         for y in range(cy):
             out[y] = raw[i, pl.ds(y, cx, stride=cy), :]
-
-    for a in range(pairs):
-        cext[a, OV : OV + cxc, :] = coef[:, a * 128 : (a + 1) * 128]
 
     @pl.when(jnp.logical_not(has_left))
     def _():
@@ -181,6 +189,9 @@
     start(p_halo(0))
     to_planes(1, qf.at[1])
     start(q_halo(0))
+    coef_load.wait()
+    for a in range(pairs):
+        cext[a, OV : OV + cxc, :] = coef[:, a * 128 : (a + 1) * 128]
     coef_rims = beside(
         cext.at[:, cxc : cxc + OV, :], cext.at[:, :OV, :],
         cext.at[:, OV : 2 * OV, :], cext.at[:, OV + cxc :, :], ce_s, ce_r,
@@ -215,7 +226,7 @@
 
         lax.fori_loop(0, cy // 2, body, 0, unroll=2)
 
-    def with_rim(halo, lap, use):
+    def with_rim(halo, lap, use, out, keep):
         def body(i, carry):
             y0 = 2 * i
             y1 = y0 + 1
@@ -228,8 +239,13 @@
             )
             ox = dot(rim_x[...], jnp.concatenate(split(edge), 0))
             ox = ox[:cx] + ox[cx:]
-            use(y0, lap[y0] + ox[:, :cz])
-            use(y1, lap[y1] + ox[:, cz:])
+            laps = (lap[y0] + ox[:, :cz], lap[y1] + ox[:, cz:])
+            nexts = [use(y, value) for y, value in zip((y0, y1), laps)]
+            for y, value, new in zip((y0, y1), laps, nexts):
+                if keep is not None:
+                    keep[y] = value
+                if new is not None:
+                    out[y] = new
             return carry
 
         lax.fori_loop(0, cy // 2, body, 0, unroll=2)
@@ -268,6 +284,8 @@
     lax.fori_loop(0, cy, source, 0, unroll=2)
     to_planes(2, pf.at[0])
     to_planes(3, qf.at[0])
+    for copy in matrix_loads:
+        copy.wait()
     finish(coef_rims)
     expand(cext, sig)
 
@@ -285,17 +303,16 @@
         scale = wave[t]
 
         def use_p(y, lap):
-            lp[t, y] = lap
-            pf[t + 2, y] = 2.0 * pf[t + 1, y] - pf[t, y] + sig2[y] * lap + scale * src[y]
-
-        with_rim(ph.at[t], lp.at[t], use_p)
+            return 2.0 * pf[t + 1, y] - pf[t, y] + sig2[y] * lap + scale * src[y]
+
+        with_rim(ph.at[t], lp.at[t], use_p, pf.at[t + 2], lp.at[t])
         start(p_halo(t + 1))
         finish(q_halo(t))
 
         def use_q(y, lap):
-            qf[t + 2, y] = 2.0 * qf[t + 1, y] - qf[t, y] + sig2[y] * lap
-
-        with_rim(qh.at[t], lq, use_q)
+            return 2.0 * qf[t + 1, y] - qf[t, y] + sig2[y] * lap
+
+        with_rim(qh.at[t], lq, use_q, qf.at[t + 2], None)
 
         @pl.when(t < steps - 1)
         def _():
@@ -358,10 +375,7 @@
         scatter.append(copy)
     finish(p_halo(steps))
 
-    def keep(y, lap):
-        lp[steps, y] = lap
-
-    with_rim(ph.at[steps], lp.at[steps], keep)
+    with_rim(ph.at[steps], lp.at[steps], lambda y, lap: None, None, lp.at[steps])
     mine = part[shot]
     for d in range(1, n_shot):
         scatter[d - 1].wait()
@@ -372,11 +386,35 @@
         copy = peer_copy(tot.at[shot], tot.at[shot], d, ag_s, ag_r)
         copy.start()
         gather.append(copy)
+    squares = jnp.zeros((8, 128), F32)
+    first = lax.rem(shot, halfs) * rows
+    for g in range(group):
+        for r in range(0, rows, 8):
+            inside = jnp.logical_and(first + r >= OV, first + r < OV + cxc)
+            value = mine[g, r : r + 8] * jnp.where(inside, 1.0, 0.0).astype(F32)
+            squares = squares + value * mine[g, r : r + 8]
+    sq_out[...] = squares
+    sums = []
+    for d in range(1, n_tile):
+        copy = pltpu.make_async_remote_copy(
+            src_ref=sq_out, dst_ref=sq_in.at[d - 1], send_sem=sq_s.at[d - 1], recv_sem=sq_r.at[d - 1],
+            device_id={"tile": lax.rem(tile + d, n_tile)}, device_id_type=MESH,
+        )
+        copy.start()
+        sums.append(copy)
+    for d in range(1, n_tile):
+        sums[d - 1].wait()
+        squares = squares + sq_in[d - 1]
+    sq_all[shot] = squares
+    sums = []
+    for d in range(1, n_shot):
+        copy = peer_copy(sq_all.at[shot], sq_all.at[shot], d, sa_s, sa_r)
+        copy.start()
+        sums.append(copy)
     for copy in gather:
         copy.wait()
     left_on = jnp.where(has_left, 1.0, 0.0).astype(F32)
     right_on = jnp.where(has_right, 1.0, 0.0).astype(F32)
-    squares = jnp.zeros((8, 128), F32)
     for a in range(pairs):
         pieces = []
         for r in range(halfs):
@@ -386,22 +424,12 @@
         ttot[a, :OV, :] = whole[:OV] * left_on
         ttot[a, OV : OV + cxc, :] = whole[OV : OV + cxc]
         ttot[a, OV + cxc :, :] = whole[OV + cxc :] * right_on
-        for r in range(OV, OV + cxc, 8):
-            squares = squares + whole[r : r + 8] * whole[r : r + 8]
-    sq_out[...] = squares
-    sums = []
-    for d in range(1, n_tile):
-        copy = pltpu.make_async_remote_copy(
-            src_ref=sq_out, dst_ref=sq_in.at[d - 1], send_sem=sq_s.at[d - 1], recv_sem=sq_r.at[d - 1],
-            device_id={"tile": lax.rem(tile + d, n_tile)}, device_id_type=MESH,
-        )
-        copy.start()
-        sums.append(copy)
     expand(ttot, exp_t)
     for copy in sums:
         copy.wait()
-    for d in range(1, n_tile):
-        squares = squares + sq_in[d - 1]
+    squares = sq_all[0]
+    for d in range(1, n_shot):
+        squares = squares + sq_all[d]
     cells = float(n_tile * cxc * 2 * pairs * 64)
     mean = jnp.sum(jnp.sum(squares, axis=0, keepdims=True), axis=1, keepdims=True) / cells
     scale = 1.0 / jnp.sqrt(mean + EPSILON)
@@ -440,10 +468,10 @@
             jax.ShapeDtypeStruct((cxc, merged), F32),
             jax.ShapeDtypeStruct((cx * cy, cz), F32),
         ),
-        in_specs=[pl.BlockSpec(memory_space=pl.ANY)] * 4
-        + [vmem] * 3
+        in_specs=[pl.BlockSpec(memory_space=pltpu.HBM)] * 5
+        + [vmem] * 2
         + [pl.BlockSpec(memory_space=pltpu.SMEM)]
-        + [vmem] * len(consts),
+        + [pl.BlockSpec(memory_space=pltpu.HBM)] * len(consts),
         out_specs=(vmem, vmem),
         scratch_shapes=[
             buf(4, cx * cy, cz), sem(4),
@@ -460,9 +488,12 @@
             sem(max(1, n_shot - 1)), sem(max(1, n_shot - 1)),
             sem(max(1, n_shot - 1)), sem(max(1, n_shot - 1)),
             sem(max(1, n_tile - 1)), sem(max(1, n_tile - 1)),
-        ],
+            buf(n_shot, 8, 128), sem(max(1, n_shot - 1)), sem(max(1, n_shot - 1)),
+            sem(1 + len(consts)), buf(cxc, merged),
+        ]
+        + [pltpu.VMEM(c.shape, c.dtype) for c in consts],
         compiler_params=pltpu.CompilerParams(
-            collective_id=0, has_side_effects=True, vmem_limit_bytes=56 * 1024 * 1024
+            collective_id=0, has_side_effects=True, vmem_limit_bytes=38 * 1024 * 1024
         ),
     )(
         flat(p_now), flat(p_prev), flat(adj_now), flat(adj_next), coef_old,

time: 52.7 us -> 61.1 us (1.16)
  local copies, waits for them, and re-layouts: 3.83 us -> 14.2 us
  Pallas kernels: 48.1 us -> 45.7 us
    unnamed x2 -> x32, local copies, waits for them, and re-layouts: 3.83 us -> 14.2 us
    pallas_call x1, Pallas kernels: 48.1 us -> 45.7 us  [on_device(): pl.pallas_call(functools.partial(kernel, dims, n_shot, n_tile, spline_y),...]
where the time goes in v1:
time: 61.1 us; the launch traced here: 60.6 us
  Pallas kernels  45.7 us (75%)
  local copies, waits for them, and re-layouts  14.2 us (23%)
  between operations  0.68 us (1%)
    pallas_call x1, Pallas kernels, on_device(): pl.pallas_call(functools.partial(kernel, dims, n_shot, n_tile, spline_y),...  45.7 us
    unnamed x32, local copies, waits for them, and re-layouts  14.2 us

profile of v1, /device:TPU:0, one launch (start us, length us, event | category | flops | bytes accessed | tf_op | source)
XLA Modules:
  0.0 60.6 jit_solution(12196099304292323378)
XLA Ops:
  0.6 0.0 copy-start.12
  0.6 0.0 copy-start.13
  0.7 0.0 copy-start.14
  0.7 0.6 %copy-done.12 = s32[1,64]{1,0:T(1,128)S(1)} copy-done((s32[1,64]{1,0:T(1,128)S(1)}, s32[1,64]{1,0:T(1,128)}, u32[]{:S(2)}) %copy-start.12) | copy-done | bytes 280
  1.3 0.0 copy-done.13
  1.3 0.0 copy-done.14
  1.3 0.0 copy-start
  1.3 1.2 %copy-done = f32[1,128,16,128]{3,2,1,0:T(8,128)S(1)} copy-done((f32[1,128,16,128]{3,2,1,0:T(8,128)S(1)}, f32[1,128,16,128]{3,2,1,0:T(8,128)}, u32[]{:S(2)}) %copy-start) | copy-done | bytes 1048600
  2.5 0.0 copy-start.1
  2.5 1.2 %copy-done.1 = f32[1,128,16,128]{3,2,1,0:T(8,128)S(1)} copy-done((f32[1,128,16,128]{3,2,1,0:T(8,128)S(1)}, f32[1,128,16,128]{3,2,1,0:T(8,128)}, u32[]{:S(2)}) %copy-start.1) | copy-done | bytes 1048600
  3.8 0.0 copy-start.2
  3.8 1.2 %copy-done.2 = f32[1,128,16,128]{3,2,1,0:T(8,128)S(1)} copy-done((f32[1,128,16,128]{3,2,1,0:T(8,128)S(1)}, f32[1,128,16,128]{3,2,1,0:T(8,128)}, u32[]{:S(2)}) %copy-start.2) | copy-done | bytes 1048600
  5.0 0.0 copy-start.3
  5.0 1.2 %copy-done.3 = f32[1,128,16,128]{3,2,1,0:T(8,128)S(1)} copy-done((f32[1,128,16,128]{3,2,1,0:T(8,128)S(1)}, f32[1,128,16,128]{3,2,1,0:T(8,128)}, u32[]{:S(2)}) %copy-start.3) | copy-done | bytes 1048600
  6.2 0.0 copy-start.4
  6.2 0.9 %copy-done.4 = f32[64,512]{1,0:T(8,128)S(1)} copy-done((f32[64,512]{1,0:T(8,128)S(1)}, f32[64,512]{1,0:T(8,128)}, u32[]{:S(2)}) %copy-start.4) | copy-done | bytes 131096
  7.1 0.0 copy-start.5
  7.1 0.9 %copy-done.5 = f32[256,128]{1,0:T(8,128)S(1)} copy-done((f32[256,128]{1,0:T(8,128)S(1)}, f32[256,128]{1,0:T(8,128)}, u32[]{:S(2)}) %copy-start.5) | copy-done | bytes 131096
  8.0 0.0 copy-start.6
  8.0 0.9 %copy-done.6 = f32[128,256]{1,0:T(8,128)S(1)} copy-done((f32[128,256]{1,0:T(8,128)S(1)}, f32[128,256]{1,0:T(8,128)}, u32[]{:S(2)}) %copy-start.6) | copy-done | bytes 131096
  8.9 0.0 copy-start.7
  8.9 0.9 %copy-done.7 = bf16[256,256]{1,0:T(8,128)(2,1)S(1)} copy-done((bf16[256,256]{1,0:T(8,128)(2,1)S(1)}, bf16[256,256]{1,0:T(8,128)(2,1)}, u32[]{:S(2)}) %copy-start.7) | copy-done | bytes 131096
  9.8 0.0 copy-start.8
  9.8 0.9 %copy-done.8 = bf16[256,256]{1,0:T(8,128)(2,1)S(1)} copy-done((bf16[256,256]{1,0:T(8,128)(2,1)S(1)}, bf16[256,256]{1,0:T(8,128)(2,1)}, u32[]{:S(2)}) %copy-start.8) | copy-done | bytes 131096
  10.7 0.0 copy-start.9
  10.7 0.8 %copy-done.9 = f32[128,80]{1,0:T(8,128)S(1)} copy-done((f32[128,80]{1,0:T(8,128)S(1)}, f32[128,80]{1,0:T(8,128)}, u32[]{:S(2)}) %copy-start.9) | copy-done | bytes 40984
  11.6 0.0 copy-start.10
  11.6 0.8 %copy-done.10 = bf16[256,32]{1,0:T(8,128)(2,1)S(1)} copy-done((bf16[256,32]{1,0:T(8,128)(2,1)S(1)}, bf16[256,32]{1,0:T(8,128)(2,1)}, u32[]{:S(2)}) %copy-start.10) | copy-done | bytes 16408
  12.4 0.0 copy-start.11
  12.4 0.8 %copy-done.11 = f32[80,128]{1,0:T(8,128)S(1)} copy-done((f32[80,128]{1,0:T(8,128)S(1)}, f32[80,128]{1,0:T(8,128)}, u32[]{:S(2)}) %copy-start.11) | copy-done | bytes 40984
  13.2 45.7 %shard_map.158 = (f32[64,512]{1,0:T(8,128)S(1)}, f32[2048,128]{1,0:T(8,128)S(1)}) custom-call(f32[2048,128]{1,0:T(8,128)S(1)} %bitcast.7, f32[2048,128]{1,0:T(8,128)S(1)} %bitcast.8, f32[2048,128]{1,0:T(8,128)S(1)} %bitcast.9, f32[2048,128]{1,0:T(8,128)S(1)} %bitcast.10, f32[64,512]{1,0:T(8,128)S(1)} %copy-done.4, s32[1,64]{1,0:T(1,128)S(1)} %copy-done.12, ...), custom_call_target="tpu_custom_call" | custom-call | tf_op jit(solution)/shard_map/pallas_call | solution.py:465
  58.9 0.7 %copy.19 = f32[64,512]{1,0:T(8,128)} copy(f32[64,512]{1,0:T(8,128)S(1)} %get-tuple-element.8) | data formatting | bytes 262144
  59.6 1.0 %copy.20 = f32[1,128,16,128]{3,2,1,0:T(8,128)} copy(f32[1,128,16,128]{3,2,1,0:T(8,128)S(1)} %bitcast.6) | data formatting | bytes 2097152
Async XLA Ops:
  0.6 0.7 %copy-start.12 = (s32[1,64]{1,0:T(1,128)S(1)}, s32[1,64]{1,0:T(1,128)}, u32[]{:S(2)}) copy-start(s32[1,64]{1,0:T(1,128)} %signs.1) | copy-start | bytes 772
  0.6 0.7 %copy-start.13 = (s32[64]{0:T(128)S(1)}, s32[64]{0:T(128)}, u32[]{:S(2)}) copy-start(s32[64]{0:T(128)} %param.21) | copy-start | bytes 772
  0.7 0.7 %copy-start.14 = (f32[5]{0:T(128)S(1)}, f32[5]{0:T(128)}, u32[]{:S(2)}) copy-start(f32[5]{0:T(128)} %wave.1) | copy-start | bytes 64
  1.3 1.2 %copy-start = (f32[1,128,16,128]{3,2,1,0:T(8,128)S(1)}, f32[1,128,16,128]{3,2,1,0:T(8,128)}, u32[]{:S(2)}) copy-start(f32[1,128,16,128]{3,2,1,0:T(8,128)} %param.15) | copy-start | bytes 3145732
  2.5 1.2 %copy-start.1 = (f32[1,128,16,128]{3,2,1,0:T(8,128)S(1)}, f32[1,128,16,128]{3,2,1,0:T(8,128)}, u32[]{:S(2)}) copy-start(f32[1,128,16,128]{3,2,1,0:T(8,128)} %param.16) | copy-start | bytes 3145732
  3.8 1.2 %copy-start.2 = (f32[1,128,16,128]{3,2,1,0:T(8,128)S(1)}, f32[1,128,16,128]{3,2,1,0:T(8,128)}, u32[]{:S(2)}) copy-start(f32[1,128,16,128]{3,2,1,0:T(8,128)} %param.17) | copy-start | bytes 3145732
  5.0 1.2 %copy-start.3 = (f32[1,128,16,128]{3,2,1,0:T(8,128)S(1)}, f32[1,128,16,128]{3,2,1,0:T(8,128)}, u32[]{:S(2)}) copy-start(f32[1,128,16,128]{3,2,1,0:T(8,128)} %param.18) | copy-start | bytes 3145732
  6.2 0.9 %copy-start.4 = (f32[64,512]{1,0:T(8,128)S(1)}, f32[64,512]{1,0:T(8,128)}, u32[]{:S(2)}) copy-start(f32[64,512]{1,0:T(8,128)} %coef_in.1) | copy-start | bytes 393220
  7.1 0.9 %copy-start.5 = (f32[256,128]{1,0:T(8,128)S(1)}, f32[256,128]{1,0:T(8,128)}, u32[]{:S(2)}) copy-start(f32[256,128]{1,0:T(8,128)} %constant.20.clone.pro_z_in) | copy-start | bytes 393220
  8.0 0.9 %copy-start.6 = (f32[128,256]{1,0:T(8,128)S(1)}, f32[128,256]{1,0:T(8,128)}, u32[]{:S(2)}) copy-start(f32[128,256]{1,0:T(8,128)} %constant.18.clone.exp_z_in) | copy-start | bytes 393220
  8.9 0.9 %copy-start.7 = (bf16[256,256]{1,0:T(8,128)(2,1)S(1)}, bf16[256,256]{1,0:T(8,128)(2,1)}, u32[]{:S(2)}) copy-start(bf16[256,256]{1,0:T(8,128)(2,1)} %constant.16.clone.core_z_in) | copy-start | bytes 393220
  9.8 0.9 %copy-start.8 = (bf16[256,256]{1,0:T(8,128)(2,1)S(1)}, bf16[256,256]{1,0:T(8,128)(2,1)}, u32[]{:S(2)}) copy-start(bf16[256,256]{1,0:T(8,128)(2,1)} %constant.14.clone.core_x_in) | copy-start | bytes 393220
  10.7 0.8 %copy-start.9 = (f32[128,80]{1,0:T(8,128)S(1)}, f32[128,80]{1,0:T(8,128)}, u32[]{:S(2)}) copy-start(f32[128,80]{1,0:T(8,128)} %constant.17.clone.exp_x_in) | copy-start | bytes 122884
  11.6 0.8 %copy-start.10 = (bf16[256,32]{1,0:T(8,128)(2,1)S(1)}, bf16[256,32]{1,0:T(8,128)(2,1)}, u32[]{:S(2)}) copy-start(bf16[256,32]{1,0:T(8,128)(2,1)} %constant.15.clone.rim_x_in) | copy-start | bytes 49156
  12.4 0.8 %copy-start.11 = (f32[80,128]{1,0:T(8,128)S(1)}, f32[80,128]{1,0:T(8,128)}, u32[]{:S(2)}) copy-start(f32[80,128]{1,0:T(8,128)} %constant.19.clone.pro_x_in) | copy-start | bytes 122884

commit v2 on v1

--- a/solution.py
+++ b/solution.py
@@ -459,6 +459,7 @@
     flat = lambda v: v.reshape(cx * cy, cz)
     consts = [jnp.asarray(c) for c in constants(cx, cz, cxc, czc)]
     vmem = pl.BlockSpec(memory_space=pltpu.VMEM)
+    held = lambda v: pltpu.with_memory_space_constraint(v, pltpu.HBM)
     field = (cy, cx, cz)
     buf = lambda *shape: pltpu.VMEM(shape, F32)
     sem = lambda *shape: pltpu.SemaphoreType.DMA(shape)
@@ -496,8 +497,8 @@
             collective_id=0, has_side_effects=True, vmem_limit_bytes=38 * 1024 * 1024
         ),
     )(
-        flat(p_now), flat(p_prev), flat(adj_now), flat(adj_next), coef_old,
-        signs, elem_index.reshape(1, -1), wavelet, *consts,
+        *map(held, (flat(p_now), flat(p_prev), flat(adj_now), flat(adj_next), coef_old)),
+        signs, elem_index.reshape(1, -1), wavelet, *map(held, consts),
     )
     return direction, p_last.reshape(1, cx, cy, cz)
 

time: 61.1 us -> 48.8 us (0.80)
  local copies, waits for them, and re-layouts: 14.2 us -> 2.29 us
    unnamed x32 -> x8, local copies, waits for them, and re-layouts: 14.2 us -> 2.29 us
where the time goes in v2:
time: 48.8 us; the launch traced here: 48.6 us
  Pallas kernels  45.7 us (94%)
  local copies, waits for them, and re-layouts  2.29 us (5%)
  between operations  0.67 us (1%)
    pallas_call x1, Pallas kernels, on_device(): pl.pallas_call(functools.partial(kernel, dims, n_shot, n_tile, spline_y),...  45.7 us
    unnamed x8, local copies, waits for them, and re-layouts  2.29 us

profile of v2, /device:TPU:0, one launch (start us, length us, event | category | flops | bytes accessed | tf_op | source)
XLA Modules:
  0.0 48.6 jit_solution(2001029674451837499)
XLA Ops:
  0.6 0.0 copy-start
  0.6 0.0 copy-start.1
  0.7 0.0 copy-start.2
  0.7 0.6 %copy-done = s32[1,64]{1,0:T(1,128)S(1)} copy-done((s32[1,64]{1,0:T(1,128)S(1)}, s32[1,64]{1,0:T(1,128)}, u32[]{:S(2)}) %copy-start) | copy-done | bytes 280
  1.3 0.0 copy-done.1
  1.3 0.0 copy-done.2
  1.3 45.7 %shard_map.158 = (f32[64,512]{1,0:T(8,128)S(1)}, f32[2048,128]{1,0:T(8,128)S(1)}) custom-call(f32[2048,128]{1,0:T(8,128)} %bitcast.8, f32[2048,128]{1,0:T(8,128)} %bitcast.9, f32[2048,128]{1,0:T(8,128)} %bitcast.10, f32[2048,128]{1,0:T(8,128)} %bitcast.11, f32[64,512]{1,0:T(8,128)} %coef_in.1, s32[1,64]{1,0:T(1,128)S(1)} %copy-done, s32[1,64]{1,0:T(1,128)S(1)} %bitcast.7, ...), custom_call_target="tpu_custom_call" | custom-call | tf_op jit(solution)/shard_map/pallas_call | solution.py:466
  47.0 0.7 %copy.19 = f32[64,512]{1,0:T(8,128)} copy(f32[64,512]{1,0:T(8,128)S(1)} %get-tuple-element.8) | data formatting | bytes 262144
  47.7 1.0 %copy.20 = f32[1,128,16,128]{3,2,1,0:T(8,128)} copy(f32[1,128,16,128]{3,2,1,0:T(8,128)S(1)} %bitcast.6) | data formatting | bytes 2097152
Async XLA Ops:
  0.6 0.7 %copy-start = (s32[1,64]{1,0:T(1,128)S(1)}, s32[1,64]{1,0:T(1,128)}, u32[]{:S(2)}) copy-start(s32[1,64]{1,0:T(1,128)} %signs.1) | copy-start | bytes 772
  0.6 0.7 %copy-start.1 = (s32[64]{0:T(128)S(1)}, s32[64]{0:T(128)}, u32[]{:S(2)}) copy-start(s32[64]{0:T(128)} %param.21) | copy-start | bytes 772
  0.7 0.7 %copy-start.2 = (f32[5]{0:T(128)S(1)}, f32[5]{0:T(128)}, u32[]{:S(2)}) copy-start(f32[5]{0:T(128)} %wave.1) | copy-start | bytes 64
